TPU v7x, 512 devices: a whole 4x8x8 slice. The times are simulated.
512 devices in a mesh: row: 32 (over y_hi, z), col: 16 (over x, y_lo, core).
Axes of the slice: x: 4, y: 8 (y_hi: 4, y_lo: 2; y = y_hi * 2 + y_lo), z: 8, core: 2. Of those that a mesh axis runs over, the one named last changes fastest.
Arguments:
- anc_inverse: bfloat16 [1, 32, 256, 2, 16, 256], P(None, 'row', None, None, 'col'), may hold values from -6 to 6
- factor_one: bfloat16 [1, 32, 256, 2, 16, 256], P(None, 'row', None, None, 'col'), may hold values from -0.0625 to 0.0625
- factor_two: bfloat16 [1, 32, 256, 1, 16, 256], P(None, 'row', None, None, 'col'), may hold values from -0.0625 to 0.0625
- parent_block: bfloat16 [1, 16, 256, 256], P(None, 'col'), may hold values from -0.375 to 0.375
- diag_one: float32 [2, 16, 256, 256], P(None, 'col'), may hold values from -6 to 6
- diag_two: float32 [1, 16, 256, 256], P(None, 'col'), may hold values from -6 to 6
- pattern_one: int32 [1, 32, 2, 16], P(None, 'row', None, 'col'), may hold values from 0 to 1
- pattern_two: int32 [1, 32, 1, 16], P(None, 'row', None, 'col'), may hold values from 0 to 1, as said below
- parent: int32 [1, 16], P(None, 'col'), may hold values from 0 to 31, as said below
Outputs:
- inv_one: bfloat16 [1, 32, 256, 2, 16, 256], P(None, 'row', None, None, 'col')
- diag_inv_one: float32 [2, 16, 256, 256], P(None, 'col')
- inv_two: bfloat16 [1, 32, 256, 1, 16, 256], P(None, 'row', None, None, 'col')
- parent_inv: bfloat16 [1, 16, 256, 256], P(None, 'col')
- diag_inv_two: float32 [1, 16, 256, 256], P(None, 'col')
Inputs may be any that keep to these rules, and one draw needn't show every extreme that they name: pattern_two[J, K] is zero wherever pattern_one[J, P(K)] is zero. parent[k, c] is a level-one supernode whose index leaves remainder c when divided by 16.
All inputs are finite; a program needn't handle non-finite values.
Results may differ from a plain program's by a relative error of at most 0.007.
Values may be sent and summed in bfloat16 or wider, within the bound.
A program may use at most 64 MiB of HBM per device.

v0:
```python
import jax
import jax.numpy as jnp
from jax import lax
from jax.sharding import PartitionSpec as P


def rows_step(whole_anc, anc_rows, block):

    def add_rows(total, piece, start):
        count = piece.shape[1]
        left = whole_anc.reshape(anc_rows * block, anc_rows * count * block)
        right = piece.reshape(anc_rows * count * block, piece.shape[3] * block)
        return jnp.dot(left, right, preferred_element_type=jnp.float32)

    return add_rows


def body(
    anc_inverse,
    factor_one,
    factor_two,
    parent_block,
    diag_one,
    diag_two,
    pattern_one,
    pattern_two,
    parent,
):
    anc_rows = anc_inverse.shape[0]
    block = anc_inverse.shape[2]
    first_count = factor_one.shape[3]
    second_count = factor_two.shape[3]
    grid_rows = lax.axis_size("row")
    grid_cols = lax.axis_size("col")
    first_factor = factor_one * pattern_one.astype(jnp.bfloat16)[:, :, None, :, :, None]
    second_factor = factor_two * pattern_two.astype(jnp.bfloat16)[:, :, None, :, :, None]
    first_empty = jnp.zeros((anc_rows * block, first_count * block), jnp.float32)
    second_empty = jnp.zeros((anc_rows * block, second_count * block), jnp.float32)
    whole_anc = lax.all_gather(anc_inverse, "col", axis=4, tiled=True).reshape(
        anc_rows * block, anc_rows, grid_rows, block
    )
    add_rows = rows_step(whole_anc, anc_rows, block)
    first_total = add_rows(
        first_empty, lax.all_gather(first_factor, "row", axis=1, tiled=True), jnp.int32(0)
    )
    first_shape = (anc_rows, block, first_count, block)
    second_shape = (anc_rows, block, second_count, block)
    first_keep = pattern_one.astype(jnp.float32)
    second_keep = pattern_two.astype(jnp.float32)
    first_inv = (-first_total.reshape(first_shape) * first_keep).astype(jnp.bfloat16)
    first_cols = first_factor.reshape(first_shape)
    second_cols = second_factor.reshape(second_shape)
    diag_part = jnp.einsum(
        "ixky,ixkz->kyz", first_cols, first_inv, preferred_element_type=jnp.float32
    )
    local_parent = parent.reshape(second_count) // grid_cols
    parent_cols = jnp.take(first_inv, local_parent, axis=2)
    cross_part = jnp.einsum(
        "ixky,ixkz->kyz", parent_cols, second_cols, preferred_element_type=jnp.float32
    )
    diag_sum, cross_sum = lax.psum((diag_part, cross_part), "row")
    first_diag = diag_one.reshape(first_count, block, block) - diag_sum
    parent_diag = jnp.take(first_diag.astype(jnp.bfloat16), local_parent, axis=0)
    coupling = parent_block.reshape(second_count, block, block)
    parent_inv = (
        -(
            jnp.einsum("kyx,kxz->kyz", parent_diag, coupling, preferred_element_type=jnp.float32)
            + cross_sum
        )
    ).astype(jnp.bfloat16)
    second_total = add_rows(
        second_empty, lax.all_gather(second_factor, "row", axis=1, tiled=True), jnp.int32(0)
    )
    side = jnp.einsum("ixky,kyz->ixkz", parent_cols, coupling, preferred_element_type=jnp.float32)
    second_inv = (-(second_total.reshape(second_shape) + side) * second_keep).astype(jnp.bfloat16)
    child_part = jnp.einsum(
        "ixky,ixkz->kyz", second_cols, second_inv, preferred_element_type=jnp.float32
    )
    child_sum = lax.psum(child_part.astype(jnp.bfloat16), "row").astype(jnp.float32)
    parent_terms = jnp.einsum(
        "kxy,kxz->kyz", coupling, parent_inv, preferred_element_type=jnp.float32
    )
    second_diag = diag_two.reshape(second_count, block, block) - (child_sum + parent_terms)
    return (
        first_inv.reshape(factor_one.shape),
        first_diag.reshape(diag_one.shape),
        second_inv.reshape(factor_two.shape),
        parent_inv.reshape(parent_block.shape),
        second_diag.reshape(diag_two.shape),
    )


def solution(mesh):
    placed = (
        P(None, "row", None, None, "col", None),
        P(None, "row", None, None, "col", None),
        P(None, "row", None, None, "col", None),
        P(None, "col", None, None),
        P(None, "col", None, None),
        P(None, "col", None, None),
        P(None, "row", None, "col"),
        P(None, "row", None, "col"),
        P(None, "col"),
    )
    return jax.shard_map(
        body,
        mesh=mesh,
        in_specs=placed,
        out_specs=(
            P(None, "row", None, None, "col", None),
            P(None, "col", None, None),
            P(None, "row", None, None, "col", None),
            P(None, "col", None, None),
            P(None, "col", None, None),
        ),
        check_vma=False,
    )
```

profile of v0, /device:TPU:40, one launch (start us, length us, event | category | flops | bytes accessed | tf_op | source)
XLA Modules:
  0.0 917.3 jit_solution(8874706373367763510)
XLA Ops:
  7.2 0.0 all-gather.4.cloned.1.call-start
  7.2 0.7 convert_bitcast_fusion
  8.0 1.7 copy_multiply_fusion
  9.7 0.0 all-gather.4.cloned.1.call-update
  9.7 0.0 all-gather.6.cloned.1.call-start
  9.8 1.8 copy.41
  11.6 0.0 all-gather.6.cloned.1.call-update
  11.6 0.0 all-gather.8.cloned.1.call-start
  12.3 1.6 bitcast_multiply_fusion
  13.9 0.0 all-reduce.6.cloned.1.call-start
  14.6 0.6 dynamic-slice.9
  15.2 138.5 %all-gather.4.cloned.1.call-done = bf16[1,32,256,2,1,256]{5,2,4,3,0,1:T(8,128)(2,1)} async-done(((bf16[1,1,256,2,1,256]{5,2,4,3,0,1:T(8,128)(2,1)}), bf16[1,32,256,2,1,256]{5,2,4,3,0,1:T(8,128)(2,1)}) %all-gather.4.cloned.1.call-update) | async-done | bytes 8388624 | tf_op jit(solution)/shard_map/all_gather | solution.py:44
  153.7 14.6 %copy.40 = bf16[1,32,256,2,1,256]{2,1,5,3,4,0:T(8,128)(2,1)} copy(bf16[1,32,256,2,1,256]{5,2,4,3,0,1:T(8,128)(2,1)} %all-gather.4.cloned.1.call-done) | data formatting | bytes 16777216 | tf_op jit(solution)/shard_map/all_gather | solution.py:44
  168.4 16.5 %copy.53 = bf16[64,8,32,256]{3,1,2,0:T(8,128)(2,1)} copy(bf16[64,8,32,256]{3,2,1,0:T(8,128)(2,1)} %bitcast.112) | data formatting | bytes 16777216
  184.8 12.1 %all-gather.6.cloned.1.call-done = bf16[1,1,256,2,16,256]{2,5,4,3,1,0:T(8,128)(2,1)} async-done(((bf16[1,1,256,2,1,256]{2,5,4,3,1,0:T(8,128)(2,1)}), bf16[1,1,256,2,16,256]{2,5,4,3,1,0:T(8,128)(2,1)}) %all-gather.6.cloned.1.call-update) | async-done | bytes 4194320 | tf_op jit(solution)/shard_map/all_gather | solution.py:39
  196.9 7.2 convolution_negate_fusion
  204.1 0.2 copy.43
  204.3 1.5 convolution_bitcast_fusion.1
  205.8 1.1 fusion.11
  207.0 0.0 all-reduce.4.cloned.1.call-start
  207.0 94.3 %all-gather.8.cloned.1.call-done = bf16[1,32,256,1,1,256]{5,2,4,3,0,1:T(8,128)(2,1)} async-done(((bf16[1,1,256,1,1,256]{5,2,4,3,0,1:T(8,128)(2,1)}), bf16[1,32,256,1,1,256]{5,2,4,3,0,1:T(8,128)(2,1)}) %all-gather.8.cloned.1.call-update) | async-done | bytes 4194320 | tf_op jit(solution)/shard_map/all_gather | solution.py:72
  301.3 4.8 convolution_bitcast_fusion.4
  306.1 0.2 copy.42
  306.4 0.9 fusion.9
  307.2 0.8 copy.49
  308.0 0.9 fusion.10
  308.9 0.9 multiply_convert_fusion.1
  309.9 309.2 %all-reduce.6.cloned.1.call-done = (f32[2,256,256]{2,1,0:T(8,128)}, f32[1,256,256]{2,1,0:T(8,128)}) async-done(((f32[2,256,256]{2,1,0:T(8,128)}, f32[1,256,256]{2,1,0:T(8,128)}), (f32[2,256,256]{2,1,0:T(8,128)}, f32[1,256,256]{2,1,0:T(8,128)})) %all-reduce.6.cloned.1.call-update) | async-done | bytes 786448 | tf_op jit(solution)/shard_map/psum | solution.py:61
  619.1 1.1 bitcast_subtract_fusion
  620.2 1.3 fusion.8
  621.6 287.4 %all-reduce.4.cloned.1.call-done = bf16[1,256,256]{2,1,0:T(8,128)(2,1)} async-done(((bf16[1,256,256]{2,1,0:T(8,128)(2,1)}), bf16[1,256,256]{2,1,0:T(8,128)(2,1)}) %all-reduce.4.cloned.1.call-update) | async-done | bytes 131088 | tf_op jit(solution)/shard_map/psum | solution.py:79
  909.0 1.8 fusion.7
  (17 shorter events, 0.1 us)
Async XLA Ops:
  7.2 299.2 %copy-start = (bf16[1,1,256,256]{3,2,1,0:T(8,128)(2,1)S(1)}, bf16[1,1,256,256]{3,2,1,0:T(8,128)(2,1)}, u32[]{:S(2)}) copy-start(bf16[1,1,256,256]{3,2,1,0:T(8,128)(2,1)} %param.12) | copy-start | bytes 393220
  7.2 146.6 %all-gather.4.cloned.1.call-start = ((), (), s32[]{:S(2)}) async-start(), calls=%async_computation | async-start | bytes 8650752 | tf_op jit(solution)/shard_map/all_gather | solution.py:44
  9.7 187.2 %all-gather.6.cloned.1.call-start = ((), (), s32[]{:S(2)}) async-start(), calls=%async_computation.1 | async-start | bytes 4456448 | tf_op jit(solution)/shard_map/all_gather | solution.py:39
  11.6 289.7 %all-gather.8.cloned.1.call-start = ((), (), s32[]{:S(2)}) async-start(), calls=%async_computation.2 | async-start | bytes 4325376 | tf_op jit(solution)/shard_map/all_gather | solution.py:72
  13.9 605.2 %all-reduce.6.cloned.1.call-start = ((), (), s32[]{:S(2)}) async-start(), calls=%async_computation.4 | async-start | bytes 1572864 | tf_op jit(solution)/shard_map/psum | solution.py:61
  196.9 7.4 copy-start.2
  196.9 8.9 copy-start.1
  207.0 702.0 %all-reduce.4.cloned.1.call-start = ((), (), s32[]{:S(2)}) async-start(), calls=%async_computation.3 | async-start | bytes 262144 | tf_op jit(solution)/shard_map/psum | solution.py:79
  301.3 317.8 %copy-start.4 = (f32[2,1,256,256]{3,2,1,0:T(8,128)S(1)}, f32[2,1,256,256]{3,2,1,0:T(8,128)}, u32[]{:S(2)}) copy-start(f32[2,1,256,256]{3,2,1,0:T(8,128)} %param.13) | copy-start | bytes 1572868
  306.1 602.9 %copy-start.6 = (f32[1,1,256,256]{3,2,1,0:T(8,128)S(1)}, f32[1,1,256,256]{3,2,1,0:T(8,128)}, u32[]{:S(2)}) copy-start(f32[1,1,256,256]{3,2,1,0:T(8,128)} %param.14) | copy-start | bytes 786436
  620.2 290.6 %copy-start.3 = (f32[2,256,256]{2,1,0:T(8,128)}, f32[2,256,256]{2,1,0:T(8,128)S(1)}, u32[]{:S(2)}) copy-start(f32[2,256,256]{2,1,0:T(8,128)S(1)} %bitcast_subtract_fusion) | copy-start | bytes 1572868
  621.5 289.3 %copy-start.5 = (bf16[1,256,256]{2,1,0:T(8,128)(2,1)}, bf16[1,256,256]{2,1,0:T(8,128)(2,1)S(1)}, u32[]{:S(2)}) copy-start(bf16[1,256,256]{2,1,0:T(8,128)(2,1)S(1)} %fusion.8) | copy-start | bytes 393220
Sparse Core Ops, SparseCore 0:
  11.8 141.9 all-gather.3
  156.4 40.4 all-gather.5
  200.7 100.6 all-gather.7
  304.7 314.3 all-reduce.5
  622.7 286.2 all-reduce.3
where the time goes:
time: 918 us; the launch traced here: 917 us
  waiting for transfers between devices  842 us (92%)
  local copies, waits for them, and re-layouts  34.7 us (4%)
  matrix products  19.5 us (2%)
  between operations  15.2 us (2%)
    psum x1, waiting for transfers between devices, body(): diag_sum, cross_sum = lax.psum((diag_part, cross_part), 'row')  309 us
    psum x1, waiting for transfers between devices, body(): lax.psum(child_part.astype(jnp.bfloat16), 'row').astype(jnp.float32)  287 us
    all_gather x1, waiting for transfers between devices, body(): lax.all_gather(first_factor, 'row', axis=1, tiled=True)  139 us
    all_gather x1, waiting for transfers between devices, body(): lax.all_gather(second_factor, 'row', axis=1, tiled=True)  94.3 us
    unnamed x17, local copies, waits for them, and re-layouts  19.1 us
  transfers between devices with their start and end apart: 5, of which 5 were waited for; matrix products, arithmetic and copies ran while one was open for 6% of the time, Pallas kernels for 0%

commit v1 on v0

--- a/solution.py
+++ b/solution.py
@@ -76,7 +76,11 @@
     child_part = jnp.einsum(
         "ixky,ixkz->kyz", second_cols, second_inv, preferred_element_type=jnp.float32
     )
-    child_sum = lax.psum(child_part.astype(jnp.bfloat16), "row").astype(jnp.float32)
+
+    def proceed_skins(xin):
+        return jnp.sum(lax.all_gather(xin, axis_name="row"), axis=0)
+
+    child_sum = proceed_skins(child_part.astype(jnp.bfloat16)).astype(jnp.float32)
     parent_terms = jnp.einsum(
         "kxy,kxz->kyz", coupling, parent_inv, preferred_element_type=jnp.float32
     )

time: 918 us -> 735 us (0.80)
  the two profiles are of different devices: /device:TPU:40 before, /device:TPU:2 now
where the time goes in v1:
time: 735 us
  waiting for transfers between devices  657 us (89%)
  local copies, waits for them, and re-layouts  35.8 us (5%)
  matrix products  17.9 us (2%)
  between operations  15.2 us (2%)
  other arithmetic  8.89 us (1%)
    psum x1, waiting for transfers between devices, body(): diag_sum, cross_sum = lax.psum((diag_part, cross_part), 'row')  309 us
    all_gather x1, waiting for transfers between devices, body(): lax.all_gather(first_factor, 'row', axis=1, tiled=True)  140 us
    all_gather x1, waiting for transfers between devices, proceed_skins(): return jnp.sum(lax.all_gather(xin, axis_name='row'), axis=0)  99.8 us
    all_gather x1, waiting for transfers between devices, body(): lax.all_gather(second_factor, 'row', axis=1, tiled=True)  96.9 us
    unnamed x19, local copies, waits for them, and re-layouts  20.1 us
  transfers between devices with their start and end apart: 5, of which 5 were waited for; matrix products, arithmetic and copies ran while one was open for 8% of the time, Pallas kernels for 0%

profile of v1, /device:TPU:2, one launch (start us, length us, event | category | flops | bytes accessed | tf_op | source)
XLA Modules:
  0.0 734.7 jit_solution(6466807105872588584)
XLA Ops:
  7.2 0.7 convert_bitcast_fusion
  8.0 1.7 copy_multiply_fusion
  9.7 0.0 all-gather.8.cloned.1.call-start
  9.8 1.8 copy.45
  12.3 1.6 bitcast_multiply_fusion
  13.9 0.0 all-reduce.3.cloned.1.call-start
  14.6 0.6 dynamic-slice.9
  15.2 140.2 %all-gather.6.cloned.1.call-done = bf16[1,32,256,2,1,256]{5,2,4,3,0,1:T(8,128)(2,1)} async-done(((bf16[1,1,256,2,1,256]{5,2,4,3,0,1:T(8,128)(2,1)}), bf16[1,32,256,2,1,256]{5,2,4,3,0,1:T(8,128)(2,1)}) %all-gather.6.cloned.1.call-update) | async-done | bytes 8388624 | tf_op jit(solution)/shard_map/all_gather | solution.py:44
  155.5 14.6 %copy.44 = bf16[1,32,256,2,1,256]{2,1,5,3,4,0:T(8,128)(2,1)} copy(bf16[1,32,256,2,1,256]{5,2,4,3,0,1:T(8,128)(2,1)} %all-gather.6.cloned.1.call-done) | data formatting | bytes 16777216 | tf_op jit(solution)/shard_map/all_gather | solution.py:44
  170.1 16.5 %copy.58 = bf16[64,8,32,256]{3,1,2,0:T(8,128)(2,1)} copy(bf16[64,8,32,256]{3,2,1,0:T(8,128)(2,1)} %bitcast.109) | data formatting | bytes 16777216
  186.6 10.4 %all-gather.8.cloned.1.call-done = bf16[1,1,256,2,16,256]{2,5,4,3,1,0:T(8,128)(2,1)} async-done(((bf16[1,1,256,2,1,256]{2,5,4,3,1,0:T(8,128)(2,1)}), bf16[1,1,256,2,16,256]{2,5,4,3,1,0:T(8,128)(2,1)}) %all-gather.8.cloned.1.call-update) | async-done | bytes 4194320 | tf_op jit(solution)/shard_map/all_gather | solution.py:39
  197.0 7.2 convolution_negate_fusion
  204.2 0.2 copy.47
  204.4 1.5 convolution_bitcast_fusion.1
  205.9 1.1 fusion.10
  207.0 0.0 all-gather.12.cloned.1.call-start
  207.1 96.9 %all-gather.10.cloned.1.call-done = bf16[1,32,256,1,1,256]{5,2,4,3,0,1:T(8,128)(2,1)} async-done(((bf16[1,1,256,1,1,256]{5,2,4,3,0,1:T(8,128)(2,1)}), bf16[1,32,256,1,1,256]{5,2,4,3,0,1:T(8,128)(2,1)}) %all-gather.10.cloned.1.call-update) | async-done | bytes 4194320 | tf_op jit(solution)/shard_map/all_gather | solution.py:72
  303.9 4.8 convolution_bitcast_fusion.4
  308.7 0.9 fusion.9
  309.7 0.9 convolution_convert_fusion
  310.6 0.1 copy.51
  310.7 0.2 copy.46
  311.0 0.8 copy.54
  311.7 0.9 multiply_convert_fusion.1
  312.7 309.2 %all-reduce.3.cloned.1.call-done = (f32[2,256,256]{2,1,0:T(8,128)}, f32[1,256,256]{2,1,0:T(8,128)}) async-done(((f32[2,256,256]{2,1,0:T(8,128)}, f32[1,256,256]{2,1,0:T(8,128)}), (f32[2,256,256]{2,1,0:T(8,128)}, f32[1,256,256]{2,1,0:T(8,128)})) %all-reduce.3.cloned.1.call-update) | async-done | bytes 786448 | tf_op jit(solution)/shard_map/psum | solution.py:61
  621.9 1.1 bitcast_subtract_fusion
  623.0 1.3 fusion.8
  624.4 99.8 %all-gather.12.cloned.1.call-done = bf16[8192,256]{1,0:T(8,128)(2,1)} async-done(((bf16[256,256]{1,0:T(8,128)(2,1)}), bf16[8192,256]{1,0:T(8,128)(2,1)}) %all-gather.12.cloned.1.call-update) | async-done | bytes 4194320 | tf_op jit(solution)/shard_map/all_gather | solution.py:81
  724.2 2.8 reduce.2
  727.0 0.1 copy.52
  727.1 0.2 fusion.2
  727.3 0.8 copy.55
  (21 shorter events, 0.2 us)
Async XLA Ops:
  7.2 301.6 %copy-start = (bf16[1,1,256,256]{3,2,1,0:T(8,128)(2,1)S(1)}, bf16[1,1,256,256]{3,2,1,0:T(8,128)(2,1)}, u32[]{:S(2)}) copy-start(bf16[1,1,256,256]{3,2,1,0:T(8,128)(2,1)} %param.12) | copy-start | bytes 393220
  7.2 148.3 %all-gather.6.cloned.1.call-start = ((), (), s32[]{:S(2)}) async-start(), calls=%async_computation | async-start | bytes 8650752 | tf_op jit(solution)/shard_map/all_gather | solution.py:44
  9.7 187.3 %all-gather.8.cloned.1.call-start = ((), (), s32[]{:S(2)}) async-start(), calls=%async_computation.1 | async-start | bytes 4456448 | tf_op jit(solution)/shard_map/all_gather | solution.py:39
  11.6 292.3 %all-gather.10.cloned.1.call-start = ((), (), s32[]{:S(2)}) async-start(), calls=%async_computation.2 | async-start | bytes 4325376 | tf_op jit(solution)/shard_map/all_gather | solution.py:72
  13.9 608.0 %all-reduce.3.cloned.1.call-start = ((), (), s32[]{:S(2)}) async-start(), calls=%async_computation.4 | async-start | bytes 1572864 | tf_op jit(solution)/shard_map/psum | solution.py:61
  197.0 7.4 %copy-start.2 = (bf16[1,1,256,1,1,256]{5,2,4,3,0,1:T(8,128)(2,1)S(1)}, bf16[1,1,256,1,1,256]{5,2,4,3,0,1:T(8,128)(2,1)}, u32[]{:S(2)}) copy-start(bf16[1,1,256,1,1,256]{5,2,4,3,0,1:T(8,128)(2,1)} %bitcast_multiply_fusion) | copy-start | bytes 393220
  197.0 8.9 %copy-start.1 = (bf16[1,1,256,2,1,256]{5,2,4,3,0,1:T(8,128)(2,1)S(1)}, bf16[1,1,256,2,1,256]{5,2,4,3,0,1:T(8,128)(2,1)}, u32[]{:S(2)}) copy-start(bf16[1,1,256,2,1,256]{5,2,4,3,0,1:T(8,128)(2,1)} %copy_multiply_fusion) | copy-start | bytes 786436
  207.0 517.2 %all-gather.12.cloned.1.call-start = ((), (), s32[]{:S(2)}) async-start(), calls=%async_computation.3 | async-start | bytes 4325376 | tf_op jit(solution)/shard_map/all_gather | solution.py:81
  303.9 6.7 copy-start.6
  308.7 313.2 %copy-start.4 = (f32[2,1,256,256]{3,2,1,0:T(8,128)S(1)}, f32[2,1,256,256]{3,2,1,0:T(8,128)}, u32[]{:S(2)}) copy-start(f32[2,1,256,256]{3,2,1,0:T(8,128)} %param.13) | copy-start | bytes 1572868
  623.0 105.2 %copy-start.3 = (f32[2,256,256]{2,1,0:T(8,128)}, f32[2,256,256]{2,1,0:T(8,128)S(1)}, u32[]{:S(2)}) copy-start(f32[2,256,256]{2,1,0:T(8,128)S(1)} %bitcast_subtract_fusion) | copy-start | bytes 1572868
  624.4 103.8 %copy-start.5 = (bf16[1,256,256]{2,1,0:T(8,128)(2,1)}, bf16[1,256,256]{2,1,0:T(8,128)(2,1)S(1)}, u32[]{:S(2)}) copy-start(bf16[1,256,256]{2,1,0:T(8,128)(2,1)S(1)} %fusion.8) | copy-start | bytes 393220
Sparse Core Ops, SparseCore 0:
  11.8 143.6 all-gather.5
  158.1 38.8 all-gather.7
  200.7 103.1 all-gather.9
  307.3 314.5 all-reduce.2
  626.0 98.1 all-gather.11
